TPU v7x, 128 devices: a whole 4x4x4 slice. The times are simulated.
128 devices in a mesh: rep: 4 (over z_lo, core), shard: 32 (over z_hi, x, y).
Axes of the slice: x: 4, y: 4, z: 4 (z_hi: 2, z_lo: 2; z = z_hi * 2 + z_lo), core: 2. Of those that a mesh axis runs over, the one named last changes fastest.
Arguments:
- local_layers: float32 [4, 4, 768, 768], P('rep', None, 'shard'), may hold values from -6 to 6
- global_layers: float32 [4, 768, 768], P(None, 'shard'), may hold values from -6 to 6
- momentum_layers: float32 [4, 768, 768], P(None, 'shard'), may hold values from -3 to 3
- local_embed: float32 [4, 32128, 768], P('rep', 'shard'), may hold values from -6 to 6
- global_embed: float32 [32128, 768], P('shard'), may hold values from -6 to 6
- momentum_embed: float32 [32128, 768], P('shard'), may hold values from -3 to 3
- proj_basis: float32 [768, 64], replicated, may hold values from -0.21875 to 0.21875
Outputs:
- mean_layers: float32 [4, 768, 768], P(None, 'shard')
- moment_layers: float32 [4, 768, 768], P(None, 'shard')
- weights_layers: float32 [4, 768, 768], P(None, 'shard')
- copy_layers: bfloat16 [4, 768, 768], replicated
- mean_embed: float32 [32128, 768], P('shard')
- moment_embed: float32 [32128, 768], P('shard')
- weights_embed: float32 [32128, 768], P('shard')
All inputs are finite; a program needn't handle non-finite values.
Results may differ from a plain program's by a relative error of at most 0.0085.
Values may be sent and summed in bfloat16 or wider, within the bound.
A program may use at most 128 MiB of HBM per device.

v0:
```python
import jax
import jax.numpy as jnp
from jax import lax
from jax.sharding import PartitionSpec as P

OUTER_MOMENTUM = 0.9
OUTER_RATE = 0.7


def outer_update(mean_diff, momentum, weights):
    new_moment = OUTER_MOMENTUM * momentum + mean_diff
    new_weights = weights - OUTER_RATE * (mean_diff + OUTER_MOMENTUM * new_moment)
    return (new_moment, new_weights)


def body(
    local_layers,
    global_layers,
    momentum_layers,
    local_embed,
    global_embed,
    momentum_embed,
    proj_basis,
):
    groups = lax.axis_size("rep")
    layer_diff = global_layers - local_layers[0]
    mean_layers = lax.psum(layer_diff, "rep") / groups
    moment_layers, weights_layers = outer_update(mean_layers, momentum_layers, global_layers)
    copy_layers = lax.all_gather(weights_layers.astype(jnp.bfloat16), "shard", axis=1, tiled=True)
    embed_diff = global_embed - local_embed[0]
    embed_full = lax.psum(embed_diff.astype(jnp.bfloat16), "rep").astype(jnp.float32) / groups
    low_mean = jnp.dot(embed_full, proj_basis, precision=lax.Precision.HIGHEST)
    mean_embed = jnp.dot(low_mean, proj_basis.T, precision=lax.Precision.HIGHEST)
    moment_embed, weights_embed = outer_update(mean_embed, momentum_embed, global_embed)
    return (
        mean_layers,
        moment_layers,
        weights_layers,
        copy_layers,
        mean_embed,
        moment_embed,
        weights_embed,
    )


def solution(mesh):
    in_specs = (
        P("rep", None, "shard", None),
        P(None, "shard", None),
        P(None, "shard", None),
        P("rep", "shard", None),
        P("shard", None),
        P("shard", None),
        P(),
    )
    out_specs = (
        P(None, "shard", None),
        P(None, "shard", None),
        P(None, "shard", None),
        P(),
        P("shard", None),
        P("shard", None),
        P("shard", None),
    )
    return jax.shard_map(body, mesh=mesh, in_specs=in_specs, out_specs=out_specs, check_vma=False)
```

profile of v0, /device:TPU:0, one launch (start us, length us, event | category | flops | bytes accessed | tf_op | source)
XLA Modules:
  0.0 204.0 jit_solution(15389995576287154729)
XLA Ops:
  7.2 0.0 copy-start
  7.2 0.0 all-reduce.3.cloned.1.call-start
  7.2 1.8 bitcast_subtract_fusion.1
  9.1 0.0 all-reduce.3.cloned.1.call-update
  9.1 0.0 all-reduce.5.cloned.1.call-start
  9.1 4.3 %fusion = bf16[1004,768]{1,0:T(8,128)(2,1)} fusion(f32[1004,768]{1,0:T(8,128)} %param.11, f32[1,1004,768]{2,0,1:T(1,128)} %param.10), kind=kLoop, calls=%fused_computation.1 | loop fusion | flops 1542144 | bytes 7710720 | tf_op jit(solution)/shard_map/convert_element_type | solution.py:31
  13.5 0.0 copy-start.1
  13.5 0.0 all-reduce.5.cloned.1.call-update
  13.5 0.0 all-gather.2.cloned.1.call-start
  13.5 36.6 %all-reduce.3.cloned.1.call-done = f32[4,24,768]{2,1,0:T(8,128)} async-done(((f32[4,24,768]{2,1,0:T(8,128)}), f32[4,24,768]{2,1,0:T(8,128)}) %all-reduce.3.cloned.1.call-update) | async-done | bytes 294928 | tf_op jit(solution)/shard_map/psum | solution.py:27
  50.2 2.2 %fusion.6 = (bf16[4,24,768]{2,1,0:T(8,128)(2,1)}, f32[4,24,768]{2,1,0:T(8,128)}, f32[4,24,768]{2,1,0:T(8,128)}, f32[4,24,768]{2,1,0:T(8,128)}) fusion(f32[4,24,768]{2,1,0:T(8,128)} %param.8, f32[4,24,768]{2,1,0:T(8,128)} %param.9, f32[4,24,768]{2,1,0:T(8,128)} %all-reduce.3.cloned.1.call-done), kind=kLoop, calls=%fused_computation.13 | loop fusion | flops 589824 | bytes 1916928 | tf_op jit(solution)/shard_map/convert_element_type | solution.py:29
  52.3 0.0 all-gather.2.cloned.1.call-update
  52.3 50.6 %all-reduce.5.cloned.1.call-done = bf16[1004,768]{1,0:T(8,128)(2,1)} async-done(((bf16[1004,768]{1,0:T(8,128)(2,1)}), bf16[1004,768]{1,0:T(8,128)(2,1)}) %all-reduce.5.cloned.1.call-update) | async-done | bytes 1542160 | tf_op jit(solution)/shard_map/psum | solution.py:31
  103.0 0.0 copy-done
  103.0 3.9 %fusion.1 = f32[1004,64]{1,0:T(8,128)S(1)} fusion(f32[768,64]{0,1:T(8,128)S(1)} %copy-done, bf16[1004,768]{1,0:T(8,128)(2,1)} %all-reduce.5.cloned.1.call-done), kind=kOutput, calls=%fused_computation.4 | convolution fusion | flops 593725440 | bytes 1995776 | tf_op jit(solution)/shard_map/dot_general | solution.py:32
  106.9 0.0 copy-done.1
  106.9 8.7 %multiply_subtract_fusion = (f32[1004,768]{1,0:T(8,128)}, f32[1004,768]{1,0:T(8,128)}, f32[1004,768]{1,0:T(8,128)}) fusion(f32[1004,768]{1,0:T(8,128)S(1)} %copy-done.1, f32[1004,768]{1,0:T(8,128)} %param.12, f32[1004,64]{1,0:T(8,128)S(1)} %fusion.1, f32[768,64]{0,1:T(8,128)S(1)} %copy-done), kind=kOutput, calls=%fused_computation.2 | convolution fusion | flops 596809728 | bytes 15875072 | tf_op jit(solution)/shard_map/dot_general | solution.py:33
  115.6 77.1 %all-gather.2.cloned.1.call-done = bf16[4,768,768]{2,1,0:T(8,128)(2,1)} async-done(((bf16[4,24,768]{2,1,0:T(8,128)(2,1)}), bf16[4,768,768]{2,1,0:T(8,128)(2,1)}) %all-gather.2.cloned.1.call-update) | async-done | bytes 4718608 | tf_op jit(solution)/shard_map/all_gather | solution.py:29
  192.7 4.8 %copy.19 = bf16[4,768,768]{2,1,0:T(8,128)(2,1)} copy(bf16[4,768,768]{2,1,0:T(8,128)(2,1)} %all-gather.2.cloned.1.call-done) | data formatting | bytes 9437184
Async XLA Ops:
  7.2 95.8 %copy-start = (f32[768,64]{0,1:T(8,128)S(1)}, f32[768,64]{0,1:T(8,128)}, u32[]{:S(2)}) copy-start(f32[768,64]{0,1:T(8,128)} %param.13) | copy-start | bytes 589828
  7.2 43.0 %all-reduce.3.cloned.1.call-start = ((), (), s32[]{:S(2)}) async-start(), calls=%async_computation | async-start | bytes 589824 | tf_op jit(solution)/shard_map/psum | solution.py:27
  9.1 93.9 %all-reduce.5.cloned.1.call-start = ((), (), s32[]{:S(2)}) async-start(), calls=%async_computation.2 | async-start | bytes 3096576 | tf_op jit(solution)/shard_map/psum | solution.py:31
  13.5 93.4 %copy-start.1 = (f32[1004,768]{1,0:T(8,128)S(1)}, f32[1004,768]{1,0:T(8,128)}, u32[]{:S(2)}) copy-start(f32[1004,768]{1,0:T(8,128)} %param.11) | copy-start | bytes 9252868
  13.5 179.2 %all-gather.2.cloned.1.call-start = ((), (), s32[]{:S(2)}) async-start(), calls=%async_computation.1 | async-start | bytes 4866048 | tf_op jit(solution)/shard_map/all_gather | solution.py:29
Sparse Core Ops, SparseCore 0:
  11.1 39.0 all-reduce.2
  53.3 49.6 all-reduce.4
  106.6 86.0 all-gather.1
where the time goes:
time: 204 us
  waiting for transfers between devices  164 us (80%)
  between operations  13.8 us (7%)
  matrix products  12.6 us (6%)
  other arithmetic  8.33 us (4%)
  local copies, waits for them, and re-layouts  4.84 us (2%)
    all_gather x1, waiting for transfers between devices, body(): lax.all_gather(weights_layers.astype(jnp.bfloat16), 'shard', axis=1, tile...  77.1 us
    psum x1, waiting for transfers between devices, body(): lax.psum(embed_diff.astype(jnp.bfloat16), 'rep').astype(jnp.float32)  50.6 us
    psum x1, waiting for transfers between devices, body(): mean_layers = lax.psum(layer_diff, 'rep') / groups  36.6 us
    dot_general x1, matrix products, body(): jnp.dot(low_mean, proj_basis.T, precision=lax.Precision.HIGHEST)  8.67 us
    unnamed x5, local copies, waits for them, and re-layouts  4.84 us
    convert_element_type x1, other arithmetic, body(): embed_diff.astype(jnp.bfloat16)  4.34 us
  transfers between devices with their start and end apart: 3, of which 3 were waited for; matrix products, arithmetic and copies ran while one was open for 9% of the time, Pallas kernels for 0%

commit v1 on v0

--- a/solution.py
+++ b/solution.py
@@ -26,7 +26,15 @@
     layer_diff = global_layers - local_layers[0]
     mean_layers = lax.psum(layer_diff, "rep") / groups
     moment_layers, weights_layers = outer_update(mean_layers, momentum_layers, global_layers)
-    copy_layers = lax.all_gather(weights_layers.astype(jnp.bfloat16), "shard", axis=1, tiled=True)
+    copy_layers = jnp.concatenate(
+        lax.all_to_all(
+            jnp.stack([weights_layers.astype(jnp.bfloat16)] * lax.axis_size("shard"), axis=0),
+            "shard",
+            0,
+            0,
+        ),
+        axis=1,
+    )
     embed_diff = global_embed - local_embed[0]
     embed_full = lax.psum(embed_diff.astype(jnp.bfloat16), "rep").astype(jnp.float32) / groups
     low_mean = jnp.dot(embed_full, proj_basis, precision=lax.Precision.HIGHEST)

time: 204 us -> 184 us (0.902)
  waiting for transfers between devices: 164 us -> 130 us
  starting transfers between devices: 0.12 us -> 9.84 us
  local copies, waits for them, and re-layouts: 4.84 us -> 7.58 us
    all_gather x1 -> x0, waiting for transfers between devices: 77.1 us -> none  [body(): lax.all_gather(weights_layers.astype(jnp.bfloat16), 'shard', axis=1, tile...]
    psum x1, waiting for transfers between devices: 50.6 us -> 89.1 us  [body(): lax.psum(embed_diff.astype(jnp.bfloat16), 'rep').astype(jnp.float32)]
    all_to_all x0 -> x1, starting transfers between devices: none -> 9.76 us  [body(): lax.all_to_all(jnp.stack([weights_layers.astype(jnp.bfloat16)] * lax.axis...]
    all_to_all x0 -> x1, local copies, waits for them, and re-layouts: none -> 4.83 us  [body(): lax.all_to_all(jnp.stack([weights_layers.astype(jnp.bfloat16)] * lax.axis...]
    unnamed x5 -> x4, local copies, waits for them, and re-layouts: 4.84 us -> 0.01 us
    psum x1, waiting for transfers between devices: 36.6 us -> 41.1 us  [body(): mean_layers = lax.psum(layer_diff, 'rep') / groups]
    another operation x0 -> x1, local copies, waits for them, and re-layouts: none -> 2.73 us  [body(): jnp.stack([weights_layers.astype(jnp.bfloat16)] * lax.axis_size('shard'),...]
  transfers between devices with their start and end apart: 3 -> 3, of which waited for: 3 -> 2; matrix products, arithmetic and copies ran while one was open for 9% -> 9% of each run, Pallas kernels for 0% -> 0%
where the time goes in v1:
time: 184 us; the launch traced here: 182 us
  waiting for transfers between devices  130 us (71%)
  between operations  14.1 us (8%)
  matrix products  13.2 us (7%)
  starting transfers between devices  9.84 us (5%)
  local copies, waits for them, and re-layouts  7.58 us (4%)
  other arithmetic  7.34 us (4%)
    psum x1, waiting for transfers between devices, body(): lax.psum(embed_diff.astype(jnp.bfloat16), 'rep').astype(jnp.float32)  89.1 us
    psum x1, waiting for transfers between devices, body(): mean_layers = lax.psum(layer_diff, 'rep') / groups  41.1 us
    all_to_all x1, starting transfers between devices, body(): lax.all_to_all(jnp.stack([weights_layers.astype(jnp.bfloat16)] * lax.axis...  9.76 us
    dot_general x1, matrix products, body(): jnp.dot(low_mean, proj_basis.T, precision=lax.Precision.HIGHEST)  8.74 us
    all_to_all x1, local copies, waits for them, and re-layouts, body(): lax.all_to_all(jnp.stack([weights_layers.astype(jnp.bfloat16)] * lax.axis...  4.83 us
    dot_general x1, matrix products, body(): low_mean = jnp.dot(embed_full, proj_basis, precision=lax.Precision.HIGHEST)  4.47 us
  transfers between devices with their start and end apart: 3, of which 2 were waited for; matrix products, arithmetic and copies ran while one was open for 9% of the time, Pallas kernels for 0%

profile of v1, /device:TPU:0, one launch (start us, length us, event | category | flops | bytes accessed | tf_op | source)
XLA Modules:
  0.0 182.2 jit_solution(8589102730722269212)
XLA Ops:
  7.2 0.0 copy-start
  7.2 0.0 all-reduce.3.cloned.1.call-start
  7.2 1.8 %bitcast_subtract_fusion.1 = f32[4,24,768]{2,1,0:T(8,128)} fusion(f32[4,24,768]{2,1,0:T(8,128)} %param.8, f32[1,4,24,768]{3,2,1,0:T(8,128)} %param.7), kind=kLoop, calls=%fused_computation.8 | loop fusion | flops 73728 | bytes 884736 | tf_op jit(solution)/shard_map/sub | solution.py:26
  9.1 0.0 all-reduce.3.cloned.1.call-update
  9.1 41.1 %all-reduce.3.cloned.1.call-done = f32[4,24,768]{2,1,0:T(8,128)} async-done(((f32[4,24,768]{2,1,0:T(8,128)}), f32[4,24,768]{2,1,0:T(8,128)}) %all-reduce.3.cloned.1.call-update) | async-done | bytes 294928 | tf_op jit(solution)/shard_map/psum | solution.py:27
  50.2 2.1 %fusion.6 = (bf16[4,24,768]{2,1,0:T(8,128)(2,1)S(1)}, f32[4,24,768]{2,1,0:T(8,128)}, f32[4,24,768]{2,1,0:T(8,128)}, f32[4,24,768]{2,1,0:T(8,128)}) fusion(f32[4,24,768]{2,1,0:T(8,128)} %param.8, f32[4,24,768]{2,1,0:T(8,128)} %param.9, f32[4,24,768]{2,1,0:T(8,128)} %all-reduce.3.cloned.1.call-done), kind=kLoop, calls=%fused_computation.13 | loop fusion | flops 589824 | bytes 1916928 | tf_op jit(solution)/shard_map/convert_element_type | solution.py:31
  52.3 2.7 %stack.2 = bf16[32,4,24,768]{3,2,1,0:T(8,128)(2,1)} broadcast(bf16[4,24,768]{2,1,0:T(8,128)(2,1)S(1)} %get-tuple-element.9), dimensions={1,2,3} | broadcast | bytes 4866048 | tf_op jit(solution)/shard_map/stack | solution.py:31
  55.0 0.0 copy-start.1
  55.0 9.8 %all-to-all-start = ((bf16[32,4,24,768]{3,2,1,0:T(8,128)(2,1)}), bf16[32,4,24,768]{3,2,1,0:T(8,128)(2,1)}, u32[]{:S(2)}, u32[]{:S(2)}) async-start(bf16[32,4,24,768]{3,2,1,0:T(8,128)(2,1)} %stack.2), calls=%async_computation | async-start | bytes 9437184 | tf_op jit(solution)/shard_map/all_to_all | solution.py:30
  64.8 0.0 all-reduce.5.cloned.1.call-start
  64.8 0.0 copy-done.1
  64.8 3.4 %fusion = bf16[1004,768]{1,0:T(8,128)(2,1)} fusion(f32[1004,768]{1,0:T(8,128)S(1)} %copy-done.1, f32[1,1004,768]{2,0,1:T(1,128)} %param.10), kind=kLoop, calls=%fused_computation.1 | loop fusion | flops 1542144 | bytes 7710720 | tf_op jit(solution)/shard_map/convert_element_type | solution.py:39
  68.2 0.0 all-reduce.5.cloned.1.call-update
  68.3 89.1 %all-reduce.5.cloned.1.call-done = bf16[1004,768]{1,0:T(8,128)(2,1)} async-done(((bf16[1004,768]{1,0:T(8,128)(2,1)}), bf16[1004,768]{1,0:T(8,128)(2,1)}) %all-reduce.5.cloned.1.call-update) | async-done | bytes 1542160 | tf_op jit(solution)/shard_map/psum | solution.py:39
  157.3 0.0 copy-done
  157.3 4.5 %fusion.1 = f32[1004,64]{0,1:T(8,128)S(1)} fusion(f32[768,64]{0,1:T(8,128)S(1)} %copy-done, bf16[1004,768]{1,0:T(8,128)(2,1)} %all-reduce.5.cloned.1.call-done), kind=kOutput, calls=%fused_computation.4 | convolution fusion | flops 593725440 | bytes 1995776 | tf_op jit(solution)/shard_map/dot_general | solution.py:40
  161.8 8.7 %multiply_subtract_fusion = (f32[1004,768]{1,0:T(8,128)}, f32[1004,768]{1,0:T(8,128)}, f32[1004,768]{1,0:T(8,128)}) fusion(f32[1004,768]{1,0:T(8,128)S(1)} %copy-done.1, f32[1004,768]{1,0:T(8,128)} %param.12, f32[1004,64]{0,1:T(8,128)S(1)} %fusion.1, f32[768,64]{0,1:T(8,128)S(1)} %copy-done), kind=kOutput, calls=%fused_computation.2 | convolution fusion | flops 596809728 | bytes 15875072 | tf_op jit(solution)/shard_map/dot_general | solution.py:41
  170.5 0.0 all-to-all-done
  170.5 4.8 %copy.14 = bf16[32,4,24,768]{3,2,0,1:T(8,128)(2,1)} copy(bf16[32,4,24,768]{3,2,1,0:T(8,128)(2,1)} %all-to-all-done) | data formatting | bytes 9437184 | tf_op jit(solution)/shard_map/all_to_all | solution.py:30
Async XLA Ops:
  7.2 150.2 %copy-start = (f32[768,64]{0,1:T(8,128)S(1)}, f32[768,64]{0,1:T(8,128)}, u32[]{:S(2)}) copy-start(f32[768,64]{0,1:T(8,128)} %param.13) | copy-start | bytes 589828
  7.2 43.0 %all-reduce.3.cloned.1.call-start = ((), (), s32[]{:S(2)}) async-start(), calls=%async_computation.1 | async-start | bytes 589824 | tf_op jit(solution)/shard_map/psum | solution.py:27
  55.0 9.8 %copy-start.1 = (f32[1004,768]{1,0:T(8,128)S(1)}, f32[1004,768]{1,0:T(8,128)}, u32[]{:S(2)}) copy-start(f32[1004,768]{1,0:T(8,128)} %param.11) | copy-start | bytes 9252868
  55.0 115.5 %all-to-all-start = ((bf16[32,4,24,768]{3,2,1,0:T(8,128)(2,1)}), bf16[32,4,24,768]{3,2,1,0:T(8,128)(2,1)}, u32[]{:S(2)}, u32[]{:S(2)}) async-start(bf16[32,4,24,768]{3,2,1,0:T(8,128)(2,1)} %stack.2), calls=%async_computation | async-start | bytes 9437184 | tf_op jit(solution)/shard_map/all_to_all | solution.py:30
  64.8 92.5 %all-reduce.5.cloned.1.call-start = ((), (), s32[]{:S(2)}) async-start(), calls=%async_computation.2 | async-start | bytes 3096576 | tf_op jit(solution)/shard_map/psum | solution.py:39
Sparse Core Ops, SparseCore 0:
  11.1 39.0 all-reduce.2
  68.7 88.5 all-reduce.4

commit v2 on v0

--- a/solution.py
+++ b/solution.py
@@ -5,6 +5,11 @@
 
 OUTER_MOMENTUM = 0.9
 OUTER_RATE = 0.7
+
+
+def summed_here(array, axis):
+    terms = lax.all_gather(array, axis)
+    return jnp.sum(terms, axis=0)
 
 
 def outer_update(mean_diff, momentum, weights):
@@ -28,7 +33,7 @@
     moment_layers, weights_layers = outer_update(mean_layers, momentum_layers, global_layers)
     copy_layers = lax.all_gather(weights_layers.astype(jnp.bfloat16), "shard", axis=1, tiled=True)
     embed_diff = global_embed - local_embed[0]
-    embed_full = lax.psum(embed_diff.astype(jnp.bfloat16), "rep").astype(jnp.float32) / groups
+    embed_full = summed_here(embed_diff.astype(jnp.bfloat16), "rep").astype(jnp.float32) / groups
     low_mean = jnp.dot(embed_full, proj_basis, precision=lax.Precision.HIGHEST)
     mean_embed = jnp.dot(low_mean, proj_basis.T, precision=lax.Precision.HIGHEST)
     moment_embed, weights_embed = outer_update(mean_embed, momentum_embed, global_embed)

time: 204 us -> 218 us (1.069)
  waiting for transfers between devices: 164 us -> 173 us
  other arithmetic: 8.33 us -> 13.5 us
    all_gather x0 -> x1, waiting for transfers between devices: none -> 63.6 us  [summed_here(): terms = lax.all_gather(array, axis)]
    psum x1 -> x0, waiting for transfers between devices: 50.6 us -> none  [body(): lax.psum(embed_diff.astype(jnp.bfloat16), 'rep').astype(jnp.float32)]
    reduce_sum x0 -> x1, other arithmetic: none -> 5.31 us  [summed_here(): return jnp.sum(terms, axis=0)]
    all_gather x1, waiting for transfers between devices: 77.1 us -> 72.5 us  [body(): lax.all_gather(weights_layers.astype(jnp.bfloat16), 'shard', axis=1, tile...]
    unnamed x0 -> x1, other arithmetic: none -> 4.38 us
    convert_element_type x1 -> x0, other arithmetic: 4.34 us -> none  [body(): embed_diff.astype(jnp.bfloat16)]
    unnamed x5 -> x9, local copies, waits for them, and re-layouts: 4.84 us -> 4.85 us
  transfers between devices with their start and end apart: 3 -> 3, of which waited for: 3 -> 3; matrix products, arithmetic and copies ran while one was open for 9% -> 11% of each run, Pallas kernels for 0% -> 0%
where the time goes in v2:
time: 218 us
  waiting for transfers between devices  173 us (79%)
  between operations  13.8 us (6%)
  other arithmetic  13.5 us (6%)
  matrix products  12.6 us (6%)
  local copies, waits for them, and re-layouts  4.85 us (2%)
    all_gather x1, waiting for transfers between devices, body(): lax.all_gather(weights_layers.astype(jnp.bfloat16), 'shard', axis=1, tile...  72.5 us
    all_gather x1, waiting for transfers between devices, summed_here(): terms = lax.all_gather(array, axis)  63.6 us
    psum x1, waiting for transfers between devices, body(): mean_layers = lax.psum(layer_diff, 'rep') / groups  36.5 us
    dot_general x1, matrix products, body(): jnp.dot(low_mean, proj_basis.T, precision=lax.Precision.HIGHEST)  8.66 us
    reduce_sum x1, other arithmetic, summed_here(): return jnp.sum(terms, axis=0)  5.31 us
    unnamed x9, local copies, waits for them, and re-layouts  4.85 us
    unnamed x1, other arithmetic  4.38 us
  transfers between devices with their start and end apart: 3, of which 3 were waited for; matrix products, arithmetic and copies ran while one was open for 11% of the time, Pallas kernels for 0%

profile of v2, /device:TPU:0, one launch (start us, length us, event | category | flops | bytes accessed | tf_op | source)
XLA Modules:
  0.0 217.6 jit_solution(11624790620430092287)
XLA Ops:
  7.2 0.0 copy-start
  7.2 0.0 all-reduce.2.cloned.1.call-start
  7.2 1.8 bitcast_subtract_fusion.1
  9.1 0.0 all-reduce.2.cloned.1.call-update
  9.1 0.0 copy-start.2
  9.1 0.0 copy-start.3
  9.1 0.0 all-gather.7.cloned.1.call-start
  9.2 4.4 %fusion.4 = bf16[1,1004,768]{2,1,0:T(8,128)(2,1)} fusion(f32[1004,768]{1,0:T(8,128)} %param.11, f32[1,1004,768]{2,0,1:T(1,128)} %param.10), kind=kLoop, calls=%fused_computation.7 | loop fusion | flops 1542144 | bytes 7710720
  13.5 0.0 all-gather.7.cloned.1.call-update
  13.6 0.0 all-gather.5.cloned.1.call-start
  13.6 36.5 %all-reduce.2.cloned.1.call-done = f32[4,24,768]{2,1,0:T(8,128)} async-done(((f32[4,24,768]{2,1,0:T(8,128)}), f32[4,24,768]{2,1,0:T(8,128)}) %all-reduce.2.cloned.1.call-update) | async-done | bytes 294928 | tf_op jit(solution)/shard_map/psum | solution.py:32
  50.2 0.0 copy-done.2
  50.2 0.0 copy-done.3
  50.2 2.0 fusion.7
  52.1 0.0 all-gather.5.cloned.1.call-update
  52.2 0.0 copy-start.1
  52.2 63.6 %all-gather.7.cloned.1.call-done = bf16[4,1004,768]{2,1,0:T(8,128)(2,1)} async-done(((bf16[1,1004,768]{2,1,0:T(8,128)(2,1)}), bf16[4,1004,768]{2,1,0:T(8,128)(2,1)}) %all-gather.7.cloned.1.call-update) | async-done | bytes 6168592 | tf_op jit(solution)/shard_map/all_gather | solution.py:11
  115.8 5.3 %reduce_sum.12 = bf16[1004,768]{1,0:T(8,128)(2,1)} reduce(bf16[4,1004,768]{2,1,0:T(8,128)(2,1)} %all-gather.7.cloned.1.call-done, bf16[]{:T(256)} %constant.3.clone.1), dimensions={0}, to_apply=%region_1.0 | reduce | flops 2313216 | bytes 7710722 | tf_op jit(solution)/shard_map/reduce_sum | solution.py:12
  121.1 0.0 copy-done
  121.1 3.9 %fusion.1 = f32[1004,64]{1,0:T(8,128)S(1)} fusion(f32[768,64]{0,1:T(8,128)S(1)} %copy-done, bf16[1004,768]{1,0:T(8,128)(2,1)} %reduce_sum.12), kind=kOutput, calls=%fused_computation.4 | convolution fusion | flops 593725440 | bytes 1995776 | tf_op jit(solution)/shard_map/dot_general | solution.py:37
  125.0 0.0 copy-done.1
  125.0 8.7 %multiply_subtract_fusion = (f32[1004,768]{1,0:T(8,128)}, f32[1004,768]{1,0:T(8,128)}, f32[1004,768]{1,0:T(8,128)}) fusion(f32[1004,768]{1,0:T(8,128)S(1)} %copy-done.1, f32[1004,768]{1,0:T(8,128)} %param.12, f32[1004,64]{1,0:T(8,128)S(1)} %fusion.1, f32[768,64]{0,1:T(8,128)S(1)} %copy-done), kind=kOutput, calls=%fused_computation.2 | convolution fusion | flops 596809728 | bytes 15875072 | tf_op jit(solution)/shard_map/dot_general | solution.py:38
  133.7 72.5 %all-gather.5.cloned.1.call-done = bf16[4,768,768]{2,1,0:T(8,128)(2,1)} async-done(((bf16[4,24,768]{2,1,0:T(8,128)(2,1)}), bf16[4,768,768]{2,1,0:T(8,128)(2,1)}) %all-gather.5.cloned.1.call-update) | async-done | bytes 4718608 | tf_op jit(solution)/shard_map/all_gather | solution.py:34
  206.2 4.8 %copy.20 = bf16[4,768,768]{2,1,0:T(8,128)(2,1)} copy(bf16[4,768,768]{2,1,0:T(8,128)(2,1)} %all-gather.5.cloned.1.call-done) | data formatting | bytes 9437184
Async XLA Ops:
  7.2 113.9 %copy-start = (f32[768,64]{0,1:T(8,128)S(1)}, f32[768,64]{0,1:T(8,128)}, u32[]{:S(2)}) copy-start(f32[768,64]{0,1:T(8,128)} %param.13) | copy-start | bytes 589828
  7.2 43.0 %all-reduce.2.cloned.1.call-start = ((), (), s32[]{:S(2)}) async-start(), calls=%async_computation | async-start | bytes 589824 | tf_op jit(solution)/shard_map/psum | solution.py:32
  9.1 41.1 %copy-start.2 = (f32[4,24,768]{2,1,0:T(8,128)S(1)}, f32[4,24,768]{2,1,0:T(8,128)}, u32[]{:S(2)}) copy-start(f32[4,24,768]{2,1,0:T(8,128)} %param.8) | copy-start | bytes 884740
  9.1 41.1 %copy-start.3 = (f32[4,24,768]{2,1,0:T(8,128)S(1)}, f32[4,24,768]{2,1,0:T(8,128)}, u32[]{:S(2)}) copy-start(f32[4,24,768]{2,1,0:T(8,128)} %param.9) | copy-start | bytes 884740
  9.1 106.7 %all-gather.7.cloned.1.call-start = ((), (), s32[]{:S(2)}) async-start(), calls=%async_computation.2 | async-start | bytes 7741440 | tf_op jit(solution)/shard_map/all_gather | solution.py:11
  13.6 192.7 %all-gather.5.cloned.1.call-start = ((), (), s32[]{:S(2)}) async-start(), calls=%async_computation.1 | async-start | bytes 4866048 | tf_op jit(solution)/shard_map/all_gather | solution.py:34
  52.2 72.9 %copy-start.1 = (f32[1004,768]{1,0:T(8,128)S(1)}, f32[1004,768]{1,0:T(8,128)}, u32[]{:S(2)}) copy-start(f32[1004,768]{1,0:T(8,128)} %param.11) | copy-start | bytes 9252868
Sparse Core Ops, SparseCore 0:
  11.1 39.0 all-reduce.1
  52.4 63.3 all-gather.6
  119.4 86.7 all-gather.4
